TPU v7x, 32 devices: a whole 2x2x4 slice. The times are simulated.
32 devices in a mesh: group: 4 (over y, x), seq: 8 (over z, core).
Axes of the slice: x: 2, y: 2, z: 4, core: 2. Of those that a mesh axis runs over, the one named last changes fastest.
Arguments:
- tokens: bfloat16 [32, 2048, 2048], P('group', 'seq'), may hold values from -6 to 6
- image_keys: bfloat16 [32, 256, 2048], P('group', 'seq'), may hold values from -256 to 256
- image_values: bfloat16 [32, 256, 2048], P('group', 'seq'), may hold values from -18 to 18
- text_len: int32 [32], replicated, may hold values from 1 to 2048
- image_len: int32 [32], replicated, may hold values from 1 to 256
- counts: int32 [6], replicated, may hold values from 1 to 4, as said below
- old_group: int32 [6], replicated, may hold values from 0 to 3, as said below
- new_group: int32 [6], replicated, may hold values from 0 to 3, as said below
- w_query: bfloat16 [2048, 2048], replicated, may hold values from -0.125 to 0.125
- w_out: bfloat16 [2048, 2048], replicated, may hold values from -0.125 to 0.125
Outputs:
- layer_out: bfloat16 [32, 2048, 2048], P('group', 'seq')
Inputs may be any that keep to these rules, and one draw needn't show every extreme that they name: `counts`: every task has at most 4 samples, and some task has exactly 4. `old_group`: each group is the old group of at most two tasks, and no two tasks share both their old group and their new group, so at most 4 samples go from one old group to one new group. `new_group`: each group is the new group of at most two tasks.
All inputs are finite; a program needn't handle non-finite values.
Results may differ from a plain program's by a relative error of at most 0.011.
Values may be sent and summed in bfloat16 or wider, within the bound.
A program may use at most 128 MiB of HBM per device.

v0:
```python
import jax
import jax.numpy as jnp
from jax import lax
from jax.sharding import PartitionSpec as P

HEAD_DIM = 128
HALF = 4
masked_score = -1e30
norm_eps = 1e-05


def layout(counts, old_group, new_group, group_count, slot_count):
    task_order = jnp.arange(counts.shape[0], dtype=jnp.int32)
    earlier = task_order[None, :] < task_order[:, None]
    same_old = old_group[None, :] == old_group[:, None]
    same_new = new_group[None, :] == new_group[:, None]
    old_start = jnp.sum(jnp.where(earlier & same_old, counts[None, :], 0), axis=1)
    new_start = jnp.sum(jnp.where(earlier & same_new, counts[None, :], 0), axis=1)
    target = jnp.arange(group_count * slot_count, dtype=jnp.int32)
    target_group = target // slot_count
    target_slot = target % slot_count
    matches = (
        (new_group[None, :] == target_group[:, None])
        & (target_slot[:, None] >= new_start[None, :])
        & (target_slot[:, None] < (new_start + counts)[None, :])
    )
    filled = jnp.any(matches, axis=1)
    offset = target_slot - jnp.sum(jnp.where(matches, new_start[None, :], 0), axis=1)
    source_group = jnp.sum(jnp.where(matches, old_group[None, :], 0), axis=1)
    source_slot = jnp.sum(jnp.where(matches, old_start[None, :], 0), axis=1) + offset
    return (filled, source_group, source_slot, offset, old_start)


def normalize(samples_rows):
    values = samples_rows.astype(jnp.float32)
    average = jnp.mean(values, axis=-1, keepdims=True)
    centred = values - average
    variance = jnp.mean(centred * centred, axis=-1, keepdims=True)
    return (centred * lax.rsqrt(variance + norm_eps)).astype(jnp.bfloat16)


def spread_rows(source_array, source_index, wanted):
    gathered = jnp.take(source_array, source_index, axis=0)
    return jnp.where(wanted[:, None, None], gathered, jnp.zeros((), source_array.dtype))


def regroup(joined, group_index, group_count, slot_count, tables, counts, old_group, new_group):
    filled, source_group, source_slot, offset, old_start = tables
    own_first = group_index * slot_count
    filled_here = lax.dynamic_slice_in_dim(filled, own_first, slot_count)
    from_group = lax.dynamic_slice_in_dim(source_group, own_first, slot_count)
    destinations = jnp.arange(group_count, dtype=jnp.int32)
    pairing = (old_group[None, :] == group_index) & (new_group[None, :] == destinations[:, None])
    pair_first = jnp.sum(jnp.where(pairing, old_start[None, :], 0), axis=1)
    pair_amount = jnp.sum(jnp.where(pairing, counts[None, :], 0), axis=1)
    position = jnp.arange(HALF, dtype=jnp.int32)
    sending = (position[None, :] < pair_amount[:, None]).reshape(-1)
    source_index = jnp.where(sending, (pair_first[:, None] + position[None, :]).reshape(-1), 0)
    outgoing = spread_rows(joined, source_index, sending)
    incoming = lax.all_to_all(outgoing, "group", split_axis=0, concat_axis=0, tiled=True)
    chosen = from_group * HALF + lax.dynamic_slice_in_dim(offset, own_first, slot_count)
    chosen = jnp.where(filled_here, chosen, 0)
    return spread_rows(incoming, chosen, filled_here)


def cross_layer(
    samples_rows, key_rows, value_rows, text_limit, key_limit, w_query, w_out, first_row
):
    slot_count, row_count, feature_count = samples_rows.shape
    head_count = w_query.shape[1] // HEAD_DIM
    normal = normalize(samples_rows).reshape(slot_count * row_count, feature_count)
    queries = (
        jnp.dot(normal, w_query, preferred_element_type=jnp.float32) * HEAD_DIM ** (-0.5)
    ).astype(jnp.bfloat16)
    queries = queries.reshape(slot_count, row_count, head_count, HEAD_DIM)
    running_max = jnp.full((slot_count, head_count, row_count), masked_score, jnp.float32)
    piece_keys = lax.all_gather(key_rows, "seq", axis=1, tiled=True)
    piece_values = lax.all_gather(value_rows, "seq", axis=1, tiled=True)
    key_count = piece_keys.shape[1]
    head_keys = piece_keys.reshape(slot_count, key_count, head_count, HEAD_DIM)
    head_values = piece_values.reshape(slot_count, key_count, head_count, HEAD_DIM)
    scores = jnp.einsum("sqhd,skhd->shqk", queries, head_keys, preferred_element_type=jnp.float32)
    position = jnp.arange(key_count, dtype=jnp.int32)
    allowed = (position[None, :] < key_limit[:, None])[:, None, None, :]
    scores = jnp.where(allowed, scores, masked_score)
    new_max = jnp.maximum(running_max, jnp.max(scores, axis=-1))
    probs = jnp.where(allowed, jnp.exp(scores - new_max[..., None]), 0.0)
    running_sum = jnp.sum(probs, axis=-1)
    weights = probs.astype(jnp.bfloat16)
    running_ctx = jnp.einsum(
        "shqk,skhd->shqd", weights, head_values, preferred_element_type=jnp.float32
    )
    running_max, running_sum, running_ctx = (new_max, running_sum, running_ctx)
    context = running_ctx / running_sum[..., None]
    context = (
        context.transpose(0, 2, 1, 3)
        .reshape(slot_count * row_count, head_count * HEAD_DIM)
        .astype(jnp.bfloat16)
    )
    projected = jnp.dot(context, w_out, preferred_element_type=jnp.float32).reshape(
        slot_count, row_count, feature_count
    )
    row_position = first_row + jnp.arange(row_count, dtype=jnp.int32)
    kept_rows = row_position[None, :] < text_limit[:, None]
    return jnp.where(kept_rows[..., None], projected, 0.0).astype(jnp.bfloat16)


def on_device(
    tokens,
    image_keys,
    image_values,
    text_len,
    image_len,
    counts,
    old_group,
    new_group,
    w_query,
    w_out,
):
    group_count = lax.axis_size("group")
    slot_count = tokens.shape[0]
    row_count = tokens.shape[1]
    group_index = lax.axis_index("group")
    first_row = lax.axis_index("seq") * row_count
    tables = layout(counts, old_group, new_group, group_count, slot_count)
    own_first = group_index * slot_count
    text_limit = lax.dynamic_slice_in_dim(text_len, own_first, slot_count)
    key_limit = lax.dynamic_slice_in_dim(image_len, own_first, slot_count)
    attended = cross_layer(
        tokens, image_keys, image_values, text_limit, key_limit, w_query, w_out, first_row
    )
    return regroup(
        attended, group_index, group_count, slot_count, tables, counts, old_group, new_group
    )


def solution(mesh):
    in_specs = (
        P("group", "seq", None),
        P("group", "seq", None),
        P("group", "seq", None),
        P(),
        P(),
        P(),
        P(),
        P(),
        P(),
        P(),
    )
    out_specs = P("group", "seq", None)
    return jax.shard_map(
        on_device, mesh=mesh, in_specs=in_specs, out_specs=out_specs, check_vma=False
    )
```

profile of v0, /device:TPU:0, one launch (start us, length us, event | category | flops | bytes accessed | tf_op | source)
XLA Modules:
  0.0 466.5 jit_solution(17421429270864026179)
XLA Ops:
  6.5 2.9 copy.28
  9.5 0.7 all-gather.5.cloned.1.call-update
  10.2 4.7 %convert_reduce_fusion = f32[8,256]{1,0:T(8,128)S(1)} fusion(bf16[8,256,2048]{2,1,0:T(8,128)(2,1)} %param.10), kind=kLoop, calls=%fused_computation.7 | loop fusion | flops 8386560 | bytes 8396800 | tf_op jit(solution)/shard_map/reduce_sum | solution.py:36
  14.9 1.1 copy-done
  16.0 2.4 fusion.4
  18.3 2.5 fusion.5
  21.0 19.4 %fusion.21 = bf16[256,8,16,128]{3,1,2,0:T(8,128)(2,1)} fusion(bf16[2048,2048]{1,0:T(8,128)(2,1)S(1)} %bitcast.27, bf16[2048,2048]{1,0:T(8,128)(2,1)S(1)} %bitcast.31), kind=kOutput, calls=%fused_computation.27 | convolution fusion | flops 17188257792 | bytes 25165824 | tf_op jit(solution)/shard_map/dot_general | solution.py:73
  40.3 9.8 %copy.38 = bf16[256,8,16,128]{3,2,1,0:T(8,128)(2,1)} copy(bf16[256,8,16,128]{3,1,2,0:T(8,128)(2,1)} %fusion.21) | data formatting | bytes 16777216
  50.1 0.1 dynamic_slice.19
  50.2 0.1 dynamic_slice.18
  50.3 0.2 select_reduce_fusion.4
  50.5 0.2 select_reduce_fusion.6
  50.7 0.1 iota_add_fusion
  50.8 0.1 select_n.139
  50.8 0.1 add.104
  51.0 0.1 lt.144
  51.3 43.1 %all-gather.3.cloned.1.call-done = bf16[8,256,2048]{2,0,1:T(8,128)(2,1)} async-done(((bf16[8,32,2048]{2,0,1:T(8,128)(2,1)}), bf16[8,256,2048]{2,0,1:T(8,128)(2,1)}) %all-gather.3.cloned.1.call-update) | async-done | bytes 8388624 | tf_op jit(solution)/shard_map/all_gather | solution.py:77
  94.3 13.0 %copy.29 = bf16[8,256,2048]{1,2,0:T(8,128)(2,1)} copy(bf16[8,256,2048]{2,0,1:T(8,128)(2,1)} %all-gather.3.cloned.1.call-done) | data formatting | bytes 16777216 | tf_op jit(solution)/shard_map/all_gather | solution.py:77
  107.3 21.7 %select_reduce_fusion = (f32[8,16,256]{2,1,0:T(8,128)S(1)}, f32[8,16,256,256]{2,3,1,0:T(8,128)}) fusion(pred[8,256]{1,0:T(8,128)(4,1)S(1)} %iota_compare_fusion, bf16[8,256,16,128]{1,3,2,0:T(8,128)(2,1)} %bitcast.26, bf16[8,256,16,128]{3,2,1,0:T(8,128)(2,1)} %bitcast.25), kind=kOutput, calls=%fused_computation.3 | convolution fusion | flops 2164228096 | bytes 50464768 | tf_op jit(solution)/shard_map/sqhd,skhd->shqk/dot_general | solution.py:82
  129.1 14.7 %fusion = f32[8,16,256]{2,1,0:T(8,128)S(1)} fusion(f32[8,16,256,256]{2,3,1,0:T(8,128)} %get-tuple-element.18, f32[8,16,256]{2,1,0:T(8,128)S(1)} %broadcast_maximum_fusion, pred[8,256]{1,0:T(8,128)(4,1)S(1)} %iota_compare_fusion), kind=kLoop, calls=%fused_computation.4 | loop fusion | flops 33521664 | bytes 33818624 | tf_op jit(solution)/shard_map/reduce_sum | solution.py:88
  143.8 32.7 %all-gather.5.cloned.1.call-done = bf16[8,256,2048]{2,1,0:T(8,128)(2,1)} async-done(((bf16[8,32,2048]{2,1,0:T(8,128)(2,1)}), bf16[8,256,2048]{2,1,0:T(8,128)(2,1)}) %all-gather.5.cloned.1.call-update) | async-done | bytes 8388624 | tf_op jit(solution)/shard_map/all_gather | solution.py:78
  176.5 11.3 %copy.32 = bf16[8,256,2048]{1,2,0:T(8,128)(2,1)} copy(bf16[8,256,2048]{2,1,0:T(8,128)(2,1)} %all-gather.5.cloned.1.call-done) | data formatting | bytes 16777216 | tf_op jit(solution)/shard_map/all_gather | solution.py:78
  187.8 17.3 %fusion.8 = bf16[8,256,16,128]{1,3,2,0:T(8,128)(2,1)S(1)} fusion(f32[8,256,16]{1,2,0:T(8,128)S(1)} %bitcast.29, bf16[8,256,16,128]{1,3,2,0:T(8,128)(2,1)} %bitcast.28, f32[8,16,256,256]{2,3,1,0:T(8,128)} %get-tuple-element.18, f32[8,16,256]{2,1,0:T(8,128)S(1)} %broadcast_maximum_fusion, pred[8,256]{1,0:T(8,128)(4,1)S(1)} %iota_compare_fusion), kind=kOutput, calls=%fused_computation.14 | convolution fusion | flops 2189426688 | bytes 50595840 | tf_op jit(solution)/shard_map/shqk,skhd->shqd/dot_general | solution.py:90
  205.1 21.7 %select_convert_fusion = bf16[8,256,2048]{2,1,0:T(8,128)(2,1)} fusion(pred[8,256]{1,0:T(8,128)(4,1)S(1)} %broadcast_compare_fusion, bf16[8,256,2048]{1,2,0:T(8,128)(2,1)S(1)} %bitcast.32, bf16[2048,2048]{1,0:T(8,128)(2,1)} %param.19), kind=kOutput, calls=%fused_computation.16 | convolution fusion | flops 17188257792 | bytes 25167872 | tf_op jit(solution)/shard_map/dot_general | solution.py:100
  226.8 10.3 %gather_fusion = bf16[16,256,2048]{2,1,0:T(8,128)(2,1)} fusion(bf16[8,256,2048]{2,1,0:T(8,128)(2,1)} %select_convert_fusion, s32[1024]{0:T(1024)S(1)} %pad_clamp_fusion.1), kind=kCustom, calls=%fused_computation | custom fusion | bytes 33554496 | tf_op jit(solution)/shard_map/jit(_take)/gather | solution.py:43
  237.1 14.3 %select_select_fusion = bf16[16,256,2048]{2,1,0:T(8,128)(2,1)} fusion(bf16[16,256,2048]{2,1,0:T(8,128)(2,1)} %gather_fusion, pred[16]{0:T(512)(128)(4,1)S(1)} %compare_and_fusion.1, pred[16]{0:T(512)(128)(4,1)S(1)} %lt.144), kind=kLoop, calls=%fused_computation.15 | loop fusion | flops 16777216 | bytes 33554464 | tf_op jit(solution)/shard_map/jit(_where)/select_n | solution.py:44
  251.4 7.0 %all-to-all-start = ((bf16[16,256,2048]{2,1,0:T(8,128)(2,1)}), bf16[16,256,2048]{2,1,0:T(8,128)(2,1)}, u32[]{:S(2)}, u32[]{:S(2)}) async-start(bf16[16,256,2048]{2,1,0:T(8,128)(2,1)} %select_select_fusion), calls=%async_computation | async-start | bytes 33554432 | tf_op jit(solution)/shard_map/all_to_all | solution.py:60
  258.4 0.1 select_reduce_fusion.3
  258.5 0.1 compare_and_fusion.2
  258.6 182.7 %all-to-all-done = bf16[16,256,2048]{2,1,0:T(8,128)(2,1)} async-done(((bf16[16,256,2048]{2,1,0:T(8,128)(2,1)}), bf16[16,256,2048]{2,1,0:T(8,128)(2,1)}, u32[]{:S(2)}, u32[]{:S(2)}) %all-to-all-start) | async-done | bytes 16777248 | tf_op jit(solution)/shard_map/all_to_all | solution.py:60
  441.3 10.6 %gather_fusion.1 = bf16[8,256,2048]{2,1,0:T(8,128)(2,1)} fusion(bf16[16,256,2048]{2,1,0:T(8,128)(2,1)} %all-to-all-done, s32[1024]{0:T(1024)S(1)} %pad_clamp_fusion), kind=kCustom, calls=%fused_computation.1 | custom fusion | bytes 16777248 | tf_op jit(solution)/shard_map/jit(_take)/gather | solution.py:43
  451.9 7.7 %select_select_fusion.1 = bf16[8,256,2048]{2,1,0:T(8,128)(2,1)} fusion(bf16[8,256,2048]{2,1,0:T(8,128)(2,1)} %gather_fusion.1, pred[8]{0:T(512)(128)(4,1)S(1)} %get-tuple-element.11, pred[8]{0:T(512)(128)(4,1)S(1)} %get-tuple-element.13), kind=kLoop, calls=%fused_computation.26 | loop fusion | flops 8388608 | bytes 16777232 | tf_op jit(solution)/shard_map/jit(_where)/select_n | solution.py:44
  (35 shorter events, 0.5 us)
Async XLA Ops:
  6.5 87.8 %all-gather.3.cloned.1.call-start = ((), (), s32[]{:S(2)}) async-start(), calls=%async_computation.1 | async-start | bytes 9437184 | tf_op jit(solution)/shard_map/all_gather | solution.py:77
  9.4 167.1 %all-gather.5.cloned.1.call-start = ((), (), s32[]{:S(2)}) async-start(), calls=%async_computation.2 | async-start | bytes 9437184 | tf_op jit(solution)/shard_map/all_gather | solution.py:78
  10.2 5.8 %copy-start = (bf16[8,256,2048]{2,1,0:T(8,128)(2,1)S(1)}, bf16[8,256,2048]{2,1,0:T(8,128)(2,1)}, u32[]{:S(2)}) copy-start(bf16[8,256,2048]{2,1,0:T(8,128)(2,1)} %param.10) | copy-start | bytes 25165828
  16.0 4.9 %slice-start = ((s8[8388608]{0:T(1024)(128)(4,1)}), s8[4194304]{0:T(1024)(128)(4,1)S(1)}, s32[]{:S(2)}) async-start(s8[8388608]{0:T(1024)(128)(4,1)} %bitcast.30), calls=%async_computation.3 | async-start | bytes 8388608
  18.3 2.6 slice-start.1
  40.3 9.8 %copy-start.4 = (s32[32]{0:T(128)S(1)}, s32[32]{0:T(128)}, u32[]{:S(2)}) copy-start(s32[32]{0:T(128)} %param.14) | copy-start | bytes 388
  40.3 9.9 %copy-start.5 = (s32[32]{0:T(128)S(1)}, s32[32]{0:T(128)}, u32[]{:S(2)}) copy-start(s32[32]{0:T(128)} %param.13) | copy-start | bytes 388
  40.3 10.0 %copy-start.1 = (s32[6]{0:T(128)S(1)}, s32[6]{0:T(128)}, u32[]{:S(2)}) copy-start(s32[6]{0:T(128)} %param.17) | copy-start | bytes 76
  40.3 10.0 %copy-start.2 = (s32[6]{0:T(128)S(1)}, s32[6]{0:T(128)}, u32[]{:S(2)}) copy-start(s32[6]{0:T(128)} %param.16) | copy-start | bytes 76
  40.3 10.0 %copy-start.3 = (s32[6]{0:T(128)S(1)}, s32[6]{0:T(128)}, u32[]{:S(2)}) copy-start(s32[6]{0:T(128)} %param.15) | copy-start | bytes 76
  251.4 189.9 %all-to-all-start = ((bf16[16,256,2048]{2,1,0:T(8,128)(2,1)}), bf16[16,256,2048]{2,1,0:T(8,128)(2,1)}, u32[]{:S(2)}, u32[]{:S(2)}) async-start(bf16[16,256,2048]{2,1,0:T(8,128)(2,1)} %select_select_fusion), calls=%async_computation | async-start | bytes 33554432 | tf_op jit(solution)/shard_map/all_to_all | solution.py:60
Sparse Core Ops, SparseCore 0:
  9.6 84.7 all-gather.2
  95.9 80.5 all-gather.4
where the time goes:
time: 468 us; the launch traced here: 466 us
  waiting for transfers between devices  259 us (55%)
  matrix products  80.1 us (17%)
  local copies, waits for them, and re-layouts  59.4 us (13%)
  other arithmetic  47.2 us (10%)
  between operations  13.6 us (3%)
  starting transfers between devices  7 us (1%)
    all_to_all x1, waiting for transfers between devices, regroup(): lax.all_to_all(outgoing, 'group', split_axis=0, concat_axis=0, tiled=True)  183 us
    all_gather x1, waiting for transfers between devices, cross_layer(): piece_keys = lax.all_gather(key_rows, 'seq', axis=1, tiled=True)  43.1 us
    all_gather x1, waiting for transfers between devices, cross_layer(): piece_values = lax.all_gather(value_rows, 'seq', axis=1, tiled=True)  32.7 us
    select_n x2, other arithmetic, spread_rows(): jnp.where(wanted[:, None, None], gathered, jnp.zeros((), source_array.dty...  22 us
    dot_general x1, matrix products, cross_layer(): jnp.einsum('sqhd,skhd->shqk', queries, head_keys, preferred_element_type=...  21.7 us
    dot_general x1, matrix products, cross_layer(): jnp.dot(context, w_out, preferred_element_type=jnp.float32)  21.7 us
    gather x2, local copies, waits for them, and re-layouts, spread_rows(): gathered = jnp.take(source_array, source_index, axis=0)  20.9 us
    dot_general x1, matrix products, cross_layer(): jnp.dot(normal, w_query, preferred_element_type=jnp.float32)  19.4 us
  transfers between devices with their start and end apart: 3, of which 3 were waited for; matrix products, arithmetic and copies ran while one was open for 19% of the time, Pallas kernels for 0%

commit v1 on v0

--- a/solution.py
+++ b/solution.py
@@ -75,7 +75,12 @@
     queries = queries.reshape(slot_count, row_count, head_count, HEAD_DIM)
     running_max = jnp.full((slot_count, head_count, row_count), masked_score, jnp.float32)
     piece_keys = lax.all_gather(key_rows, "seq", axis=1, tiled=True)
-    piece_values = lax.all_gather(value_rows, "seq", axis=1, tiled=True)
+    ring = [value_rows]
+    for hop in range(7):
+        ring.append(lax.ppermute(ring[-1], "seq", [(dev, (dev + 1) % 8) for dev in range(8)]))
+    piece_values = jnp.roll(
+        jnp.concatenate(ring[::-1], axis=1), (lax.axis_index("seq") + 1) * ring[0].shape[1], axis=1
+    )
     key_count = piece_keys.shape[1]
     head_keys = piece_keys.reshape(slot_count, key_count, head_count, HEAD_DIM)
     head_values = piece_values.reshape(slot_count, key_count, head_count, HEAD_DIM)

time: 468 us -> 553 us (1.18)
  waiting for transfers between devices: 259 us -> 301 us
  local copies, waits for them, and re-layouts: 59.4 us -> 93 us
    ppermute x0 -> x7, waiting for transfers between devices: none -> 126 us  [cross_layer(): lax.ppermute(ring[-1], 'seq', [(dev, (dev + 1) % 8) for dev in range(8)])]
    all_gather x1, waiting for transfers between devices: 43.1 us -> 0.01 us  [cross_layer(): piece_keys = lax.all_gather(key_rows, 'seq', axis=1, tiled=True)]
    all_gather x1 -> x0, waiting for transfers between devices: 32.7 us -> none  [cross_layer(): piece_values = lax.all_gather(value_rows, 'seq', axis=1, tiled=True)]
    unnamed x18 -> x43, local copies, waits for them, and re-layouts: 13.8 us -> 38 us
    dynamic_slice x0 -> x2, local copies, waits for them, and re-layouts: none -> 19.9 us  [cross_layer(): jnp.roll(jnp.concatenate(ring[::-1], axis=1), (lax.axis_index('seq') + 1)...]
    all_gather x1 -> x0, local copies, waits for them, and re-layouts: 11.3 us -> none  [cross_layer(): piece_values = lax.all_gather(value_rows, 'seq', axis=1, tiled=True)]
    all_to_all x1, waiting for transfers between devices: 183 us -> 176 us  [regroup(): lax.all_to_all(outgoing, 'group', split_axis=0, concat_axis=0, tiled=True)]
  transfers between devices with their start and end apart: 3 -> 9, of which waited for: 3 -> 7; matrix products, arithmetic and copies ran while one was open for 19% -> 17% of each run, Pallas kernels for 0% -> 0%
where the time goes in v1:
time: 553 us; the launch traced here: 550 us
  waiting for transfers between devices  301 us (54%)
  local copies, waits for them, and re-layouts  93 us (17%)
  matrix products  83.6 us (15%)
  other arithmetic  51.1 us (9%)
  between operations  13.7 us (2%)
  starting transfers between devices  7.67 us (1%)
    all_to_all x1, waiting for transfers between devices, regroup(): lax.all_to_all(outgoing, 'group', split_axis=0, concat_axis=0, tiled=True)  176 us
    ppermute x7, waiting for transfers between devices, cross_layer(): lax.ppermute(ring[-1], 'seq', [(dev, (dev + 1) % 8) for dev in range(8)])  126 us
    unnamed x43, local copies, waits for them, and re-layouts  38 us
    dot_general x1, matrix products, cross_layer(): jnp.dot(context, w_out, preferred_element_type=jnp.float32)  23.7 us
    select_n x2, other arithmetic, spread_rows(): jnp.where(wanted[:, None, None], gathered, jnp.zeros((), source_array.dty...  22 us
    dot_general x1, matrix products, cross_layer(): jnp.dot(normal, w_query, preferred_element_type=jnp.float32)  22 us
    dot_general x1, matrix products, cross_layer(): jnp.einsum('sqhd,skhd->shqk', queries, head_keys, preferred_element_type=...  21.7 us
    gather x2, local copies, waits for them, and re-layouts, spread_rows(): gathered = jnp.take(source_array, source_index, axis=0)  20.9 us
  transfers between devices with their start and end apart: 9, of which 7 were waited for; matrix products, arithmetic and copies ran while one was open for 17% of the time, Pallas kernels for 0%

profile of v1, /device:TPU:0, one launch (start us, length us, event | category | flops | bytes accessed | tf_op | source)
XLA Modules:
  0.0 550.3 jit_solution(11566205918324224974)
XLA Ops:
  7.0 2.9 copy.28
  9.9 13.8 %collective-permute-done = bf16[8,32,2048]{2,1,0:T(8,128)(2,1)S(1)} collective-permute-done((bf16[8,32,2048]{2,1,0:T(8,128)(2,1)}, bf16[8,32,2048]{2,1,0:T(8,128)(2,1)S(1)}, u32[]{:S(2)}, u32[]{:S(2)}) %collective-permute-start) | collective-permute-done | bytes 1048608 | tf_op jit(solution)/shard_map/ppermute | solution.py:80
  23.8 38.6 %collective-permute-done.1 = bf16[8,32,2048]{2,1,0:T(8,128)(2,1)S(1)} collective-permute-done((bf16[8,32,2048]{2,1,0:T(8,128)(2,1)S(1)}, bf16[8,32,2048]{2,1,0:T(8,128)(2,1)S(1)}, u32[]{:S(2)}, u32[]{:S(2)}) %collective-permute-start.1) | collective-permute-done | bytes 1048608 | tf_op jit(solution)/shard_map/ppermute | solution.py:80
  62.4 38.6 %collective-permute-done.2 = bf16[8,32,2048]{2,1,0:T(8,128)(2,1)S(1)} collective-permute-done((bf16[8,32,2048]{2,1,0:T(8,128)(2,1)S(1)}, bf16[8,32,2048]{2,1,0:T(8,128)(2,1)S(1)}, u32[]{:S(2)}, u32[]{:S(2)}) %collective-permute-start.2) | collective-permute-done | bytes 1048608 | tf_op jit(solution)/shard_map/ppermute | solution.py:80
  101.0 4.9 convert_reduce_fusion
  106.0 5.9 %fusion.4 = f32[8,256]{1,0:T(8,128)S(1)} fusion(bf16[8,256,2048]{2,1,0:T(8,128)(2,1)} %param.10, f32[8,256]{1,0:T(8,128)S(1)} %broadcast_multiply_fusion), kind=kLoop, calls=%fused_computation.10 | loop fusion | flops 16775168 | bytes 8404992 | tf_op jit(solution)/shard_map/reduce_sum | solution.py:38
  111.9 14.8 %collective-permute-done.3 = bf16[8,32,2048]{2,1,0:T(8,128)(2,1)S(1)} collective-permute-done((bf16[8,32,2048]{2,1,0:T(8,128)(2,1)S(1)}, bf16[8,32,2048]{2,1,0:T(8,128)(2,1)S(1)}, u32[]{:S(2)}, u32[]{:S(2)}) %collective-permute-start.3) | collective-permute-done | bytes 1048608 | tf_op jit(solution)/shard_map/ppermute | solution.py:80
  126.7 2.4 fusion.5
  129.1 13.7 %collective-permute-done.4 = bf16[8,32,2048]{2,1,0:T(8,128)(2,1)} collective-permute-done((bf16[8,32,2048]{2,1,0:T(8,128)(2,1)S(1)}, bf16[8,32,2048]{2,1,0:T(8,128)(2,1)}, u32[]{:S(2)}, u32[]{:S(2)}) %collective-permute-start.4) | collective-permute-done | bytes 1048608 | tf_op jit(solution)/shard_map/ppermute | solution.py:80
  142.8 22.0 %fusion.21 = bf16[256,8,16,128]{3,1,2,0:T(8,128)(2,1)} fusion(bf16[2048,2048]{1,0:T(8,128)(2,1)S(1)} %bitcast.29, bf16[2048,2048]{1,0:T(8,128)(2,1)} %param.18), kind=kOutput, calls=%fused_computation.27 | convolution fusion | flops 17188257792 | bytes 25165824 | tf_op jit(solution)/shard_map/dot_general | solution.py:73
  165.6 9.7 %copy.38 = bf16[256,8,16,128]{3,2,1,0:T(8,128)(2,1)} copy(bf16[256,8,16,128]{3,1,2,0:T(8,128)(2,1)} %fusion.21) | data formatting | bytes 16777216
  175.9 6.0 %collective-permute-done.6 = bf16[8,32,2048]{2,1,0:T(8,128)(2,1)} collective-permute-done((bf16[8,32,2048]{2,1,0:T(8,128)(2,1)}, bf16[8,32,2048]{2,1,0:T(8,128)(2,1)}, u32[]{:S(2)}, u32[]{:S(2)}) %collective-permute-start.6) | collective-permute-done | bytes 1048608 | tf_op jit(solution)/shard_map/ppermute | solution.py:80
  181.9 2.3 constant_dynamic-update-slice_fusion.15
  184.2 2.3 constant_dynamic-update-slice_fusion.14
  186.5 2.3 constant_dynamic-update-slice_fusion.13
  188.7 2.3 constant_dynamic-update-slice_fusion.12
  191.0 2.3 constant_dynamic-update-slice_fusion.11
  196.4 2.3 constant_dynamic-update-slice_fusion.7
  200.9 2.3 constant_dynamic-update-slice_fusion.5
  208.3 8.4 %constant_dynamic-slice_fusion = bf16[8,256,2048]{2,1,0:T(8,128)(2,1)} fusion(bf16[8,512,2048]{2,1,0:T(8,128)(2,1)} %constant_dynamic-update-slice_fusion, s32[]{:T(128)S(6)} %select_n.150), kind=kLoop, calls=%fused_computation.79 | loop fusion | bytes 16777220 | tf_op jit(solution)/shard_map/jit(_roll_dynamic)/dynamic_slice | solution.py:81
  216.7 11.4 %copy.32 = bf16[8,256,2048]{1,2,0:T(8,128)(2,1)} copy(bf16[8,256,2048]{2,1,0:T(8,128)(2,1)} %constant_dynamic-slice_fusion) | data formatting | bytes 16777216 | tf_op jit(solution)/shard_map/jit(_roll_dynamic)/dynamic_slice | solution.py:81
  228.1 12.8 %copy.29 = bf16[8,256,2048]{1,2,0:T(8,128)(2,1)} copy(bf16[8,256,2048]{2,0,1:T(8,128)(2,1)} %all-gather.2.cloned.1.call-done) | data formatting | bytes 16777216 | tf_op jit(solution)/shard_map/all_gather | solution.py:77
  241.0 21.7 %select_reduce_fusion = (f32[8,16,256]{2,1,0:T(8,128)S(1)}, f32[8,16,256,256]{2,3,1,0:T(8,128)}) fusion(pred[8,256]{1,0:T(8,128)(4,1)S(1)} %iota_compare_fusion, bf16[8,256,16,128]{1,3,2,0:T(8,128)(2,1)} %bitcast.28, bf16[8,256,16,128]{3,2,1,0:T(8,128)(2,1)} %bitcast.27), kind=kOutput, calls=%fused_computation.3 | convolution fusion | flops 2164228096 | bytes 50464768 | tf_op jit(solution)/shard_map/sqhd,skhd->shqk/dot_general | solution.py:87
  262.7 15.0 %fusion = f32[8,16,256]{2,1,0:T(8,128)S(1)} fusion(f32[8,16,256,256]{2,3,1,0:T(8,128)} %get-tuple-element.18, f32[8,16,256]{2,1,0:T(8,128)S(1)} %broadcast_maximum_fusion, pred[8,256]{1,0:T(8,128)(4,1)S(1)} %iota_compare_fusion), kind=kLoop, calls=%fused_computation.4 | loop fusion | flops 33521664 | bytes 33818624 | tf_op jit(solution)/shard_map/reduce_sum | solution.py:93
  277.7 16.3 %fusion.8 = bf16[8,256,16,128]{1,3,2,0:T(8,128)(2,1)} fusion(f32[8,256,16]{1,2,0:T(8,128)S(1)} %bitcast.31, bf16[8,256,16,128]{1,3,2,0:T(8,128)(2,1)S(1)} %bitcast.30, f32[8,16,256,256]{2,3,1,0:T(8,128)} %get-tuple-element.18, f32[8,16,256]{2,1,0:T(8,128)S(1)} %broadcast_maximum_fusion, pred[8,256]{1,0:T(8,128)(4,1)S(1)} %iota_compare_fusion), kind=kOutput, calls=%fused_computation.14 | convolution fusion | flops 2189426688 | bytes 50595840 | tf_op jit(solution)/shard_map/shqk,skhd->shqd/dot_general | solution.py:95
  294.0 23.7 %select_convert_fusion = bf16[8,256,2048]{2,1,0:T(8,128)(2,1)} fusion(pred[8,256]{1,0:T(8,128)(4,1)S(1)} %broadcast_compare_fusion, bf16[8,256,2048]{1,2,0:T(8,128)(2,1)} %bitcast.32, bf16[2048,2048]{1,0:T(8,128)(2,1)} %param.19), kind=kOutput, calls=%fused_computation.16 | convolution fusion | flops 17188257792 | bytes 25167872 | tf_op jit(solution)/shard_map/dot_general | solution.py:105
  317.7 10.3 %gather_fusion = bf16[16,256,2048]{2,1,0:T(8,128)(2,1)} fusion(bf16[8,256,2048]{2,1,0:T(8,128)(2,1)} %select_convert_fusion, s32[1024]{0:T(1024)S(1)} %pad_clamp_fusion.1), kind=kCustom, calls=%fused_computation | custom fusion | bytes 33554496 | tf_op jit(solution)/shard_map/jit(_take)/gather | solution.py:43
  328.0 14.3 %select_select_fusion = bf16[16,256,2048]{2,1,0:T(8,128)(2,1)} fusion(bf16[16,256,2048]{2,1,0:T(8,128)(2,1)} %gather_fusion, pred[16]{0:T(512)(128)(4,1)S(1)} %compare_and_fusion.1, pred[16]{0:T(512)(128)(4,1)S(1)} %lt.156), kind=kLoop, calls=%fused_computation.15 | loop fusion | flops 16777216 | bytes 33554464 | tf_op jit(solution)/shard_map/jit(_where)/select_n | solution.py:44
  342.3 7.0 %all-to-all-start = ((bf16[16,256,2048]{2,1,0:T(8,128)(2,1)}), bf16[16,256,2048]{2,1,0:T(8,128)(2,1)}, u32[]{:S(2)}, u32[]{:S(2)}) async-start(bf16[16,256,2048]{2,1,0:T(8,128)(2,1)} %select_select_fusion), calls=%async_computation | async-start | bytes 33554432 | tf_op jit(solution)/shard_map/all_to_all | solution.py:60
  349.5 175.6 %all-to-all-done = bf16[16,256,2048]{2,1,0:T(8,128)(2,1)} async-done(((bf16[16,256,2048]{2,1,0:T(8,128)(2,1)}), bf16[16,256,2048]{2,1,0:T(8,128)(2,1)}, u32[]{:S(2)}, u32[]{:S(2)}) %all-to-all-start) | async-done | bytes 16777248 | tf_op jit(solution)/shard_map/all_to_all | solution.py:60
  525.1 10.6 %gather_fusion.1 = bf16[8,256,2048]{2,1,0:T(8,128)(2,1)} fusion(bf16[16,256,2048]{2,1,0:T(8,128)(2,1)} %all-to-all-done, s32[1024]{0:T(1024)S(1)} %pad_clamp_fusion), kind=kCustom, calls=%fused_computation.1 | custom fusion | bytes 16777248 | tf_op jit(solution)/shard_map/jit(_take)/gather | solution.py:43
  535.7 7.7 %select_select_fusion.1 = bf16[8,256,2048]{2,1,0:T(8,128)(2,1)} fusion(bf16[8,256,2048]{2,1,0:T(8,128)(2,1)} %gather_fusion.1, pred[8]{0:T(512)(128)(4,1)S(1)} %get-tuple-element.11, pred[8]{0:T(512)(128)(4,1)S(1)} %get-tuple-element.13), kind=kLoop, calls=%fused_computation.26 | loop fusion | flops 8388608 | bytes 16777232 | tf_op jit(solution)/shard_map/jit(_where)/select_n | solution.py:44
  (73 shorter events, 12.5 us)
Async XLA Ops:
  6.5 221.6 %all-gather.2.cloned.1.call-start = ((), (), s32[]{:S(2)}) async-start(), calls=%async_computation.1 | async-start | bytes 9437184 | tf_op jit(solution)/shard_map/all_gather | solution.py:77
  6.5 17.2 %collective-permute-start = (bf16[8,32,2048]{2,1,0:T(8,128)(2,1)}, bf16[8,32,2048]{2,1,0:T(8,128)(2,1)S(1)}, u32[]{:S(2)}, u32[]{:S(2)}) collective-permute-start(bf16[8,32,2048]{2,1,0:T(8,128)(2,1)} %param.12), channel_id=1, source_target_pairs={{0,1},{1,2},{2,3},{3,4},{4,5},{5,6},{6,7},{7,0},{8,9},{9,10},{10,1... | collective-permute-start | bytes 3145736 | tf_op jit(solution)/shard_map/ppermute | solution.py:80
  9.9 116.8 %slice-start = ((s8[8388608]{0:T(1024)(128)(4,1)}), s8[4194304]{0:T(1024)(128)(4,1)S(1)}, s32[]{:S(2)}) async-start(s8[8388608]{0:T(1024)(128)(4,1)} %bitcast.25), calls=%async_computation.2 | async-start | bytes 8388608
  23.8 38.6 %collective-permute-start.1 = (bf16[8,32,2048]{2,1,0:T(8,128)(2,1)S(1)}, bf16[8,32,2048]{2,1,0:T(8,128)(2,1)S(1)}, u32[]{:S(2)}, u32[]{:S(2)}) collective-permute-start(bf16[8,32,2048]{2,1,0:T(8,128)(2,1)S(1)} %collective-permute-done), channel_id=1, source_target_pairs={{0,1},{1,2},{2,3},{3,4},{4,5},{5,6},{6,7},{7,0},{8,9},{9,10},{10,1... | collective-permute-start | bytes 3145736 | tf_op jit(solution)/shard_map/ppermute | solution.py:80
  62.4 38.6 %collective-permute-start.2 = (bf16[8,32,2048]{2,1,0:T(8,128)(2,1)S(1)}, bf16[8,32,2048]{2,1,0:T(8,128)(2,1)S(1)}, u32[]{:S(2)}, u32[]{:S(2)}) collective-permute-start(bf16[8,32,2048]{2,1,0:T(8,128)(2,1)S(1)} %collective-permute-done.1), channel_id=1, source_target_pairs={{0,1},{1,2},{2,3},{3,4},{4,5},{5,6},{6,7},{7,0},{8,9},{9,10},{10,1... | collective-permute-start | bytes 3145736 | tf_op jit(solution)/shard_map/ppermute | solution.py:80
  101.0 28.1 %copy-start.2 = (bf16[8,32,2048]{2,1,0:T(8,128)(2,1)}, bf16[8,32,2048]{2,1,0:T(8,128)(2,1)S(1)}, u32[]{:S(2)}) copy-start(bf16[8,32,2048]{2,1,0:T(8,128)(2,1)S(1)} %collective-permute-done.2) | copy-start | bytes 3145732
  101.0 25.7 %collective-permute-start.3 = (bf16[8,32,2048]{2,1,0:T(8,128)(2,1)S(1)}, bf16[8,32,2048]{2,1,0:T(8,128)(2,1)S(1)}, u32[]{:S(2)}, u32[]{:S(2)}) collective-permute-start(bf16[8,32,2048]{2,1,0:T(8,128)(2,1)S(1)} %collective-permute-done.2), channel_id=1, source_target_pairs={{0,1},{1,2},{2,3},{3,4},{4,5},{5,6},{6,7},{7,0},{8,9},{9,10},{10,1... | collective-permute-start | bytes 3145736 | tf_op jit(solution)/shard_map/ppermute | solution.py:80
  105.9 20.8 %slice-start.1 = ((s8[8388608]{0:T(1024)(128)(4,1)}), s8[4194304]{0:T(1024)(128)(4,1)S(1)}, s32[]{:S(2)}) async-start(s8[8388608]{0:T(1024)(128)(4,1)} %bitcast.25), calls=%async_computation.3 | async-start | bytes 8388608
  126.7 38.1 %copy-start.4 = (bf16[8,32,2048]{2,1,0:T(8,128)(2,1)}, bf16[8,32,2048]{2,1,0:T(8,128)(2,1)S(1)}, u32[]{:S(2)}) copy-start(bf16[8,32,2048]{2,1,0:T(8,128)(2,1)S(1)} %collective-permute-done.3) | copy-start | bytes 3145732
  126.7 16.1 %collective-permute-start.4 = (bf16[8,32,2048]{2,1,0:T(8,128)(2,1)S(1)}, bf16[8,32,2048]{2,1,0:T(8,128)(2,1)}, u32[]{:S(2)}, u32[]{:S(2)}) collective-permute-start(bf16[8,32,2048]{2,1,0:T(8,128)(2,1)S(1)} %collective-permute-done.3), channel_id=1, source_target_pairs={{0,1},{1,2},{2,3},{3,4},{4,5},{5,6},{6,7},{7,0},{8,9},{9,10},{10,1... | collective-permute-start | bytes 3145736 | tf_op jit(solution)/shard_map/ppermute | solution.py:80
  142.8 22.6 %collective-permute-start.5 = (bf16[8,32,2048]{2,1,0:T(8,128)(2,1)}, bf16[8,32,2048]{2,1,0:T(8,128)(2,1)}, u32[]{:S(2)}, u32[]{:S(2)}) collective-permute-start(bf16[8,32,2048]{2,1,0:T(8,128)(2,1)} %collective-permute-done.4), channel_id=1, source_target_pairs={{0,1},{1,2},{2,3},{3,4},{4,5},{5,6},{6,7},{7,0},{8,9},{9,10},{10,1... | collective-permute-start | bytes 3145736 | tf_op jit(solution)/shard_map/ppermute | solution.py:80
  142.8 22.0 %copy-start.6 = (s32[6]{0:T(128)S(1)}, s32[6]{0:T(128)}, u32[]{:S(2)}) copy-start(s32[6]{0:T(128)} %param.17) | copy-start | bytes 76
  142.8 22.0 %copy-start.7 = (s32[6]{0:T(128)S(1)}, s32[6]{0:T(128)}, u32[]{:S(2)}) copy-start(s32[6]{0:T(128)} %param.16) | copy-start | bytes 76
  142.8 22.0 %copy-start.8 = (s32[6]{0:T(128)S(1)}, s32[6]{0:T(128)}, u32[]{:S(2)}) copy-start(s32[6]{0:T(128)} %param.15) | copy-start | bytes 76
  164.8 10.6 %copy-start.9 = (s32[32]{0:T(128)S(1)}, s32[32]{0:T(128)}, u32[]{:S(2)}) copy-start(s32[32]{0:T(128)} %param.14) | copy-start | bytes 388
  164.8 10.6 %copy-start.10 = (s32[32]{0:T(128)S(1)}, s32[32]{0:T(128)}, u32[]{:S(2)}) copy-start(s32[32]{0:T(128)} %param.13) | copy-start | bytes 388
  164.8 30.6 %copy-start.1 = (bf16[8,32,2048]{2,1,0:T(8,128)(2,1)S(1)}, bf16[8,32,2048]{2,1,0:T(8,128)(2,1)}, u32[]{:S(2)}) copy-start(bf16[8,32,2048]{2,1,0:T(8,128)(2,1)} %param.12) | copy-start | bytes 3145732
  165.4 16.5 %collective-permute-start.6 = (bf16[8,32,2048]{2,1,0:T(8,128)(2,1)}, bf16[8,32,2048]{2,1,0:T(8,128)(2,1)}, u32[]{:S(2)}, u32[]{:S(2)}) collective-permute-start(bf16[8,32,2048]{2,1,0:T(8,128)(2,1)} %collective-permute-done.5), channel_id=1, source_target_pairs={{0,1},{1,2},{2,3},{3,4},{4,5},{5,6},{6,7},{7,0},{8,9},{9,10},{10,1... | collective-permute-start | bytes 3145736 | tf_op jit(solution)/shard_map/ppermute | solution.py:80
  175.8 27.5 %copy-start.5 = (bf16[8,32,2048]{2,1,0:T(8,128)(2,1)S(1)}, bf16[8,32,2048]{2,1,0:T(8,128)(2,1)}, u32[]{:S(2)}) copy-start(bf16[8,32,2048]{2,1,0:T(8,128)(2,1)} %copy-done.4) | copy-start | bytes 3145732
  175.8 28.5 %copy-start.3 = (bf16[8,32,2048]{2,1,0:T(8,128)(2,1)S(1)}, bf16[8,32,2048]{2,1,0:T(8,128)(2,1)}, u32[]{:S(2)}) copy-start(bf16[8,32,2048]{2,1,0:T(8,128)(2,1)} %copy-done.2) | copy-start | bytes 3145732
  262.7 15.0 %copy-start = (bf16[8,256,2048]{1,2,0:T(8,128)(2,1)S(1)}, bf16[8,256,2048]{1,2,0:T(8,128)(2,1)}, u32[]{:S(2)}) copy-start(bf16[8,256,2048]{1,2,0:T(8,128)(2,1)} %copy.32) | copy-start | bytes 25165828
  342.3 182.8 %all-to-all-start = ((bf16[16,256,2048]{2,1,0:T(8,128)(2,1)}), bf16[16,256,2048]{2,1,0:T(8,128)(2,1)}, u32[]{:S(2)}, u32[]{:S(2)}) async-start(bf16[16,256,2048]{2,1,0:T(8,128)(2,1)} %select_select_fusion), calls=%async_computation | async-start | bytes 33554432 | tf_op jit(solution)/shard_map/all_to_all | solution.py:60
Sparse Core Ops, SparseCore 0:
  10.0 111.1 all-gather.1
